TPU v7x, 128 devices: a whole 4x4x4 slice. The times are simulated.
128 devices in a mesh: row: 4 (over y), col: 32 (over z, x, core).
Axes of the slice: x: 4, y: 4, z: 4, core: 2. Of those that a mesh axis runs over, the one named last changes fastest.
Arguments:
- tokens: bfloat16 [768, 8192], P('col', 'row'), may hold values from -6 to 6
- gate_weight: bfloat16 [8192, 28672], P('row', 'col'), may hold values from -0.0625 to 0.0625
- up_weight: bfloat16 [8192, 28672], P('row', 'col'), may hold values from -0.0625 to 0.0625
- down_weight: bfloat16 [28672, 8192], P('col', 'row'), may hold values from -0.03125 to 0.03125
- mask_gate: int32 [128, 448], P('row', 'col'), may hold values from 0 to 1, as said below
- mask_up: int32 [128, 448], P('row', 'col'), may hold values from 0 to 1, as said below
- mask_down: int32 [448, 128], P('col', 'row'), may hold values from 0 to 1, as said below
- cotangent: bfloat16 [768, 8192], P('col', 'row'), may hold values from -1.5 to 1.5
Outputs:
- output: bfloat16 [768, 8192], P('col', 'row')
- grad_input: bfloat16 [768, 8192], P('col', 'row')
- grad_gate: bfloat16 [8192, 28672], P('row', 'col')
- grad_up: bfloat16 [8192, 28672], P('row', 'col')
- grad_down: bfloat16 [28672, 8192], P('col', 'row')
Inputs may be any that keep to these rules, and one draw needn't show every extreme that they name: `mask_gate`: 1 where a 64 x 64 block of the weight is kept, 0 where it is pruned. `mask_up`: 1 where a 64 x 64 block of the weight is kept, 0 where it is pruned. `mask_down`: 1 where a 64 x 64 block of the weight is kept, 0 where it is pruned.
All inputs are finite; a program needn't handle non-finite values.
Results may differ from a plain program's by a relative error of at most 0.006.
Values may be sent and summed in bfloat16 or wider, within the bound.
No kernel may reach another device: no remote copies, remote signals or barrier semaphores. Data moves between devices by JAX's collectives and lax.ppermute only.
A program may use at most 128 MiB of HBM per device.

v0:
```python
import jax
import jax.numpy as jnp
from jax import lax
from jax.sharding import PartitionSpec as P

BLOCK = 64


def expand(mask):
    return jnp.repeat(jnp.repeat(mask, BLOCK, 0), BLOCK, 1).astype(jnp.bfloat16)


def contract_last(left, right):
    return lax.dot_general(
        left, right, (((1,), (1,)), ((), ())), preferred_element_type=jnp.float32
    )


def contract_first(left, right):
    return lax.dot_general(
        left, right, (((0,), (0,)), ((), ())), preferred_element_type=jnp.float32
    )


def backward_gates(dhid, gate, up):
    sigma = jax.nn.sigmoid(gate)
    dgate = (dhid * up * sigma * (1.0 + gate * (1.0 - sigma))).astype(jnp.bfloat16)
    dup = (dhid * gate * sigma).astype(jnp.bfloat16)
    return (dgate, dup)


def body(tokens, gate_weight, up_weight, down_weight, mask_gate, mask_up, mask_down, cotangent):
    keep_gate = expand(mask_gate)
    keep_up = expand(mask_up)
    keep_down = expand(mask_down)
    w_gate = gate_weight * keep_gate
    w_up = up_weight * keep_up
    w_down = down_weight * keep_down
    width = w_gate.shape[1]
    pair = lax.all_gather(jnp.concatenate([tokens, cotangent], axis=1), "col", axis=0, tiled=True)
    depth = tokens.shape[1]
    panel = pair[:, :depth]
    cot_panel = pair[:, depth:]
    parts = jnp.concatenate(
        [
            jnp.dot(panel, w_gate, preferred_element_type=jnp.float32).astype(jnp.bfloat16),
            jnp.dot(panel, w_up, preferred_element_type=jnp.float32).astype(jnp.bfloat16),
            contract_last(cot_panel, w_down).astype(jnp.bfloat16),
        ],
        axis=1,
    )
    rows = parts.shape[0] // 4
    swapped = lax.all_to_all(parts, "row", 0, 0, tiled=True)
    total = jnp.sum(swapped.reshape(4, rows, 3 * width).astype(jnp.float32), axis=0)
    gate = total[:, :width]
    up = total[:, width : 2 * width]
    dhid = total[:, 2 * width :]
    hidden = (jax.nn.silu(gate) * up).astype(jnp.bfloat16)
    dgate, dup = backward_gates(dhid, gate, up)
    whole = lax.all_gather(jnp.concatenate([hidden, dgate, dup], axis=1), "row", axis=0, tiled=True)
    hidden = whole[:, :width]
    dgate = whole[:, width : 2 * width]
    dup = whole[:, 2 * width :]
    both = jnp.concatenate(
        [
            jnp.dot(hidden, w_down, preferred_element_type=jnp.float32).astype(jnp.bfloat16),
            (contract_last(dgate, w_gate) + contract_last(dup, w_up)).astype(jnp.bfloat16),
        ],
        axis=1,
    )
    spread = lax.all_to_all(both, "col", 0, 0, tiled=True)
    grad_down = (contract_first(hidden, cot_panel) * keep_down).astype(jnp.bfloat16)
    grad_gate = (contract_first(panel, dgate) * keep_gate).astype(jnp.bfloat16)
    grad_up = (contract_first(panel, dup) * keep_up).astype(jnp.bfloat16)
    spread = spread.reshape(-1, tokens.shape[0], 2 * depth).astype(jnp.float32)
    owned = jnp.sum(spread, axis=0).astype(jnp.bfloat16)
    output = owned[:, :depth]
    grad_input = owned[:, depth:]
    return (output, grad_input, grad_gate, grad_up, grad_down)


def solution(mesh):
    return jax.shard_map(
        body,
        mesh=mesh,
        in_specs=(
            P("col", "row"),
            P("row", "col"),
            P("row", "col"),
            P("col", "row"),
            P("row", "col"),
            P("row", "col"),
            P("col", "row"),
            P("col", "row"),
        ),
        out_specs=(
            P("col", "row"),
            P("col", "row"),
            P("row", "col"),
            P("row", "col"),
            P("col", "row"),
        ),
        check_vma=False,
    )
```

profile of v0, /device:TPU:0, one launch (start us, length us, event | category | flops | bytes accessed | tf_op | source)
XLA Modules:
  0.0 288.6 jit_solution(12454030804781257054)
XLA Ops:
  7.2 0.0 all-gather.3.cloned.1.call-start
  7.2 1.6 pad_maximum_fusion.3
  8.8 0.0 all-gather.3.cloned.1.call-update
  8.9 0.0 all-gather.5.cloned.1.call-start
  8.9 0.7 convert_element_type.88
  9.6 0.1 copy.24
  9.7 0.1 broadcast_in_dim.22
  9.9 0.1 convert_element_type.89
  10.0 0.0 copy-start.8
  10.0 6.1 %copy.25 = bf16[896,2048]{0,1:T(8,128)(2,1)} copy(bf16[896,2048]{1,0:T(8,128)(2,1)} %param.11) | data formatting | bytes 7340032 | tf_op args[3]
  16.1 0.1 broadcast_in_dim.20
  16.2 0.2 convert_element_type.85
  16.4 6.1 %copy.23 = bf16[2048,896]{0,1:T(8,128)(2,1)} copy(bf16[2048,896]{1,0:T(8,128)(2,1)} %param.10) | data formatting | bytes 7340032 | tf_op args[2]
  22.4 0.1 broadcast_in_dim.18
  22.6 0.1 convert_element_type.81
  22.7 6.1 %copy.22 = bf16[2048,896]{0,1:T(8,128)(2,1)} copy(bf16[2048,896]{1,0:T(8,128)(2,1)} %param.9) | data formatting | bytes 7340032 | tf_op args[1]
  28.8 4.4 %bitcast_multiply_fusion = bf16[896,2048]{0,1:T(8,128)(2,1)} fusion(bf16[896,2048]{0,1:T(8,128)(2,1)} %copy.25, bf16[896,32]{0,1:T(8,128)(2,1)S(1)} %convert_element_type.89), kind=kLoop, calls=%fused_computation.17 | loop fusion | flops 1835008 | bytes 7397376 | tf_op jit(solution)/shard_map/mul | solution.py:38
  33.2 2.1 bitcast_multiply_fusion.1
  35.3 1.2 copy-done.1
  36.6 2.1 bitcast_multiply_fusion.2
  38.7 23.2 %all-gather.3.cloned.1.call-done = bf16[768,4096]{1,0:T(8,128)(2,1)} async-done(((bf16[24,4096]{1,0:T(8,128)(2,1)}), bf16[768,4096]{1,0:T(8,128)(2,1)}) %all-gather.3.cloned.1.call-update) | async-done | bytes 6291472 | tf_op jit(solution)/shard_map/all_gather | solution.py:40
  61.9 6.5 %fusion.15 = bf16[768,896]{1,0:T(8,128)(2,1)S(1)} fusion(bf16[896,2048]{0,1:T(8,128)(2,1)} %bitcast_multiply_fusion, bf16[768,4096]{1,0:T(8,128)(2,1)} %all-gather.3.cloned.1.call-done), kind=kOutput, calls=%fused_computation.22 | convolution fusion | flops 2819260416 | bytes 8192000 | tf_op jit(solution)/shard_map/dot_general | solution.py:14
  68.4 3.5 %fusion.12 = bf16[768,896]{1,0:T(8,128)(2,1)S(1)} fusion(bf16[2048,896]{0,1:T(8,128)(2,1)S(1)} %copy-done.2, bf16[768,4096]{1,0:T(8,128)(2,1)S(1)} %copy-done.10), kind=kOutput, calls=%fused_computation.21 | convolution fusion | flops 2819260416 | bytes 8192000 | tf_op jit(solution)/shard_map/dot_general | solution.py:47
  71.9 3.4 %fusion.9 = bf16[768,896]{1,0:T(8,128)(2,1)S(1)} fusion(bf16[2048,896]{0,1:T(8,128)(2,1)S(1)} %copy-done.4, bf16[768,4096]{1,0:T(8,128)(2,1)S(1)} %copy-done.10), kind=kOutput, calls=%fused_computation.20 | convolution fusion | flops 2819260416 | bytes 8192000 | tf_op jit(solution)/shard_map/dot_general | solution.py:46
  75.4 0.4 pad_maximum_fusion.1
  75.7 52.6 %all_to_all.18 = bf16[4,192,2688]{2,1,0:T(8,128)(2,1)S(1)} all-to-all(bf16[4,192,2688]{2,1,0:T(8,128)(2,1)S(1)} %bitcast.21), channel_id=1, replica_groups=mesh['row'=4,'col'=32] {'row'}, dimensions={0} | all-to-all | bytes 8257536 | tf_op jit(solution)/shard_map/all_to_all | solution.py:53
  128.3 0.6 convert_reduce_fusion
  128.9 0.4 multiply_convert_fusion.5
  129.3 1.0 pad_maximum_fusion.2
  130.4 0.0 all-gather.5.cloned.1.call-update
  130.4 44.7 %all-gather.5.cloned.1.call-done = bf16[768,2688]{1,0:T(8,128)(2,1)} async-done(((bf16[192,2688]{1,0:T(8,128)(2,1)}), bf16[768,2688]{1,0:T(8,128)(2,1)}) %all-gather.5.cloned.1.call-update) | async-done | bytes 4128784 | tf_op jit(solution)/shard_map/all_gather | solution.py:60
  175.1 6.0 %convolution_convert_fusion = bf16[768,2048]{1,0:T(8,128)(2,1)S(1)} fusion(bf16[896,2048]{0,1:T(8,128)(2,1)} %bitcast_multiply_fusion, bf16[768,2688]{1,0:T(8,128)(2,1)} %all-gather.5.cloned.1.call-done), kind=kOutput, calls=%fused_computation.7 | convolution fusion | flops 2820145152 | bytes 8192000 | tf_op jit(solution)/shard_map/dot_general | solution.py:66
  181.2 3.4 %fusion.21 = f32[768,2048]{1,0:T(8,128)S(1)} fusion(bf16[2048,896]{0,1:T(8,128)(2,1)S(1)} %copy-done.5, bf16[768,2688]{1,0:T(8,128)(2,1)S(1)} %copy-done.11), kind=kOutput, calls=%fused_computation.26 | convolution fusion | flops 2818572288 | bytes 11337728 | tf_op jit(solution)/shard_map/dot_general | solution.py:14
  184.6 3.7 %add_convert_fusion = bf16[768,2048]{1,0:T(8,128)(2,1)S(1)} fusion(f32[768,2048]{1,0:T(8,128)S(1)} %fusion.21, bf16[2048,896]{0,1:T(8,128)(2,1)S(1)} %copy-done.3, bf16[768,2688]{1,0:T(8,128)(2,1)S(1)} %copy-done.11), kind=kOutput, calls=%fused_computation.5 | convolution fusion | flops 2821718016 | bytes 14483456 | tf_op jit(solution)/shard_map/dot_general | solution.py:14
  188.4 3.4 %pad_maximum_fusion = bf16[768,4096]{1,0:T(8,128)(2,1)} fusion(bf16[768,2048]{1,0:T(8,128)(2,1)S(1)} %add_convert_fusion, bf16[768,2048]{1,0:T(8,128)(2,1)S(1)} %convolution_convert_fusion), kind=kLoop, calls=%fused_computation.4 | loop fusion | flops 12582912 | bytes 12582912 | tf_op jit(solution)/shard_map/concatenate | solution.py:64
  191.8 7.6 %all-to-all-start.1 = ((bf16[32,24,4096]{2,1,0:T(8,128)(2,1)}), bf16[32,24,4096]{2,1,0:T(8,128)(2,1)}, u32[]{:S(2)}, u32[]{:S(2)}) async-start(bf16[32,24,4096]{2,1,0:T(8,128)(2,1)} %bitcast.20), calls=%async_computation.1 | async-start | bytes 12582912 | tf_op jit(solution)/shard_map/all_to_all | solution.py:71
  199.3 2.1 broadcast_in_dim.23
  201.5 6.1 %copy.28 = bf16[896,2048]{1,0:T(8,128)(2,1)} copy(bf16[896,2048]{0,1:T(8,128)(2,1)} %bitcast.22) | data formatting | bytes 7340032 | tf_op jit(solution)/shard_map/convert_element_type | solution.py:10
  207.6 2.3 broadcast_in_dim.21
  209.9 6.0 %copy.27 = bf16[2048,896]{1,0:T(8,128)(2,1)} copy(bf16[2048,896]{0,1:T(8,128)(2,1)} %bitcast.23) | data formatting | bytes 7340032 | tf_op jit(solution)/shard_map/convert_element_type | solution.py:10
  215.9 2.3 broadcast_in_dim.19
  218.2 6.2 %copy.26 = bf16[2048,896]{1,0:T(8,128)(2,1)} copy(bf16[2048,896]{0,1:T(8,128)(2,1)} %bitcast.24) | data formatting | bytes 7340032 | tf_op jit(solution)/shard_map/convert_element_type | solution.py:10
  224.4 8.5 %multiply_convert_fusion = bf16[896,2048]{1,0:T(8,128)(2,1)} fusion(bf16[896,2048]{1,0:T(8,128)(2,1)} %copy.28, bf16[768,4096]{1,0:T(8,128)(2,1)} %all-gather.3.cloned.1.call-done, bf16[768,2688]{1,0:T(8,128)(2,1)} %all-gather.5.cloned.1.call-done), kind=kOutput, calls=%fused_computation.1 | convolution fusion | flops 2824077312 | bytes 11862016 | tf_op jit(solution)/shard_map/dot_general | solution.py:20
  232.9 5.1 %multiply_convert_fusion.1 = bf16[2048,896]{1,0:T(8,128)(2,1)} fusion(bf16[2048,896]{1,0:T(8,128)(2,1)S(1)} %copy-done.6, bf16[768,4096]{1,0:T(8,128)(2,1)S(1)} %bitcast.26, bf16[768,2688]{1,0:T(8,128)(2,1)S(1)} %copy-done.12), kind=kOutput, calls=%fused_computation.2 | convolution fusion | flops 2824077312 | bytes 11862016 | tf_op jit(solution)/shard_map/dot_general | solution.py:20
  238.0 5.1 %multiply_convert_fusion.2 = bf16[2048,896]{1,0:T(8,128)(2,1)} fusion(bf16[2048,896]{1,0:T(8,128)(2,1)S(1)} %copy-done.7, bf16[768,4096]{1,0:T(8,128)(2,1)S(1)} %bitcast.26, bf16[768,2688]{1,0:T(8,128)(2,1)S(1)} %copy-done.12), kind=kOutput, calls=%fused_computation.3 | convolution fusion | flops 2824077312 | bytes 11862016 | tf_op jit(solution)/shard_map/dot_general | solution.py:20
  243.1 33.9 %all-to-all-done.1 = bf16[32,24,4096]{2,1,0:T(8,128)(2,1)} async-done(((bf16[32,24,4096]{2,1,0:T(8,128)(2,1)}), bf16[32,24,4096]{2,1,0:T(8,128)(2,1)}, u32[]{:S(2)}, u32[]{:S(2)}) %all-to-all-start.1) | async-done | bytes 6291488 | tf_op jit(solution)/shard_map/all_to_all | solution.py:71
  277.0 4.1 %reduce_sum.22 = bf16[24,4096]{1,0:T(8,128)(2,1)S(1)} reduce(bf16[32,24,4096]{2,1,0:T(8,128)(2,1)} %all-to-all-done.1, bf16[]{:T(256)} %constant.7.clone.1), dimensions={0}, to_apply=%region_1.2 | reduce | flops 3047424 | bytes 6488066 | tf_op jit(solution)/shard_map/reduce_sum | solution.py:76
  281.1 0.7 fusion.25
  (31 shorter events, 0.1 us)
Async XLA Ops:
  7.2 54.7 %all-gather.3.cloned.1.call-start = ((), (), s32[]{:S(2)}) async-start(), calls=%async_computation.2 | async-start | bytes 6488064 | tf_op jit(solution)/shard_map/all_gather | solution.py:40
  8.9 166.2 %all-gather.5.cloned.1.call-start = ((), (), s32[]{:S(2)}) async-start(), calls=%async_computation.3 | async-start | bytes 5160960 | tf_op jit(solution)/shard_map/all_gather | solution.py:60
  10.0 6.1 %copy-start.8 = (s32[32,14]{0,1:T(8,128)S(1)}, s32[32,14]{0,1:T(8,128)}, u32[]{:S(2)}) copy-start(s32[32,14]{0,1:T(8,128)} %param.13) | copy-start | bytes 5380
  16.4 6.1 %copy-start.9 = (s32[32,14]{0,1:T(8,128)S(1)}, s32[32,14]{0,1:T(8,128)}, u32[]{:S(2)}) copy-start(s32[32,14]{0,1:T(8,128)} %param.12) | copy-start | bytes 5380
  28.8 4.4 %copy-start = (bf16[2048,896]{0,1:T(8,128)(2,1)S(1)}, bf16[2048,896]{0,1:T(8,128)(2,1)}, u32[]{:S(2)}) copy-start(bf16[2048,896]{0,1:T(8,128)(2,1)} %copy.23) | copy-start | bytes 11010052
  33.2 3.4 %copy-start.1 = (bf16[2048,896]{0,1:T(8,128)(2,1)S(1)}, bf16[2048,896]{0,1:T(8,128)(2,1)}, u32[]{:S(2)}) copy-start(bf16[2048,896]{0,1:T(8,128)(2,1)} %copy.22) | copy-start | bytes 11010052
  61.9 6.5 %copy-start.2 = (bf16[2048,896]{0,1:T(8,128)(2,1)S(1)}, bf16[2048,896]{0,1:T(8,128)(2,1)}, u32[]{:S(2)}) copy-start(bf16[2048,896]{0,1:T(8,128)(2,1)} %bitcast_multiply_fusion.1) | copy-start | bytes 11010052
  61.9 6.6 %copy-start.10 = (bf16[768,4096]{1,0:T(8,128)(2,1)S(1)}, bf16[768,4096]{1,0:T(8,128)(2,1)}, u32[]{:S(2)}) copy-start(bf16[768,4096]{1,0:T(8,128)(2,1)} %all-gather.3.cloned.1.call-done) | copy-start | bytes 18874372
  68.4 3.5 %copy-start.4 = (bf16[2048,896]{0,1:T(8,128)(2,1)S(1)}, bf16[2048,896]{0,1:T(8,128)(2,1)}, u32[]{:S(2)}) copy-start(bf16[2048,896]{0,1:T(8,128)(2,1)} %bitcast_multiply_fusion.2) | copy-start | bytes 11010052
  175.1 6.1 %copy-start.5 = (bf16[2048,896]{0,1:T(8,128)(2,1)S(1)}, bf16[2048,896]{0,1:T(8,128)(2,1)}, u32[]{:S(2)}) copy-start(bf16[2048,896]{0,1:T(8,128)(2,1)} %bitcast_multiply_fusion.2) | copy-start | bytes 11010052
  175.1 6.1 %copy-start.11 = (bf16[768,2688]{1,0:T(8,128)(2,1)S(1)}, bf16[768,2688]{1,0:T(8,128)(2,1)}, u32[]{:S(2)}) copy-start(bf16[768,2688]{1,0:T(8,128)(2,1)} %all-gather.5.cloned.1.call-done) | copy-start | bytes 12386308
  181.2 3.4 %copy-start.3 = (bf16[2048,896]{0,1:T(8,128)(2,1)S(1)}, bf16[2048,896]{0,1:T(8,128)(2,1)}, u32[]{:S(2)}) copy-start(bf16[2048,896]{0,1:T(8,128)(2,1)} %bitcast_multiply_fusion.1) | copy-start | bytes 11010052
  191.8 85.2 %all-to-all-start.1 = ((bf16[32,24,4096]{2,1,0:T(8,128)(2,1)}), bf16[32,24,4096]{2,1,0:T(8,128)(2,1)}, u32[]{:S(2)}, u32[]{:S(2)}) async-start(bf16[32,24,4096]{2,1,0:T(8,128)(2,1)} %bitcast.20), calls=%async_computation.1 | async-start | bytes 12582912 | tf_op jit(solution)/shard_map/all_to_all | solution.py:71
  218.2 14.7 %slice-start = ((s8[6291456]{0:T(1024)(128)(4,1)}), s8[2097152]{0:T(1024)(128)(4,1)S(1)}, s32[]{:S(2)}) async-start(s8[6291456]{0:T(1024)(128)(4,1)} %bitcast.25), calls=%async_computation.4 | async-start | bytes 4194304
  224.4 8.5 %copy-start.6 = (bf16[2048,896]{1,0:T(8,128)(2,1)S(1)}, bf16[2048,896]{1,0:T(8,128)(2,1)}, u32[]{:S(2)}) copy-start(bf16[2048,896]{1,0:T(8,128)(2,1)} %copy.27) | copy-start | bytes 11010052
  224.4 8.5 %slice-start.1 = ((s8[6291456]{0:T(1024)(128)(4,1)}), s8[4194304]{0:T(1024)(128)(4,1)S(1)}, s32[]{:S(2)}) async-start(s8[6291456]{0:T(1024)(128)(4,1)} %bitcast.25), calls=%async_computation.5 | async-start | bytes 8388608
  224.4 8.5 %copy-start.12 = (bf16[768,2688]{1,0:T(8,128)(2,1)S(1)}, bf16[768,2688]{1,0:T(8,128)(2,1)}, u32[]{:S(2)}) copy-start(bf16[768,2688]{1,0:T(8,128)(2,1)} %all-gather.5.cloned.1.call-done) | copy-start | bytes 12386308
  232.9 5.1 %copy-start.7 = (bf16[2048,896]{1,0:T(8,128)(2,1)S(1)}, bf16[2048,896]{1,0:T(8,128)(2,1)}, u32[]{:S(2)}) copy-start(bf16[2048,896]{1,0:T(8,128)(2,1)} %copy.26) | copy-start | bytes 11010052
Sparse Core Ops, SparseCore 0:
  10.2 51.5 all-gather.2
  130.5 44.5 all-gather.4
where the time goes:
time: 290 us; the launch traced here: 289 us
  waiting for transfers between devices  102 us (35%)
  blocking collectives  52.6 us (18%)
  local copies, waits for them, and re-layouts  46.2 us (16%)
  matrix products  45.3 us (16%)
  other arithmetic  20.9 us (7%)
  between operations  14.3 us (5%)
  starting transfers between devices  7.65 us (3%)
    all_to_all x1, blocking collectives, body(): swapped = lax.all_to_all(parts, 'row', 0, 0, tiled=True)  52.6 us
    all_gather x1, waiting for transfers between devices, body(): lax.all_gather(jnp.concatenate([hidden, dgate, dup], axis=1), 'row', axis...  44.7 us
    all_to_all x1, waiting for transfers between devices, body(): spread = lax.all_to_all(both, 'col', 0, 0, tiled=True)  33.9 us
    all_gather x1, waiting for transfers between devices, body(): lax.all_gather(jnp.concatenate([tokens, cotangent], axis=1), 'col', axis=...  23.2 us
    unnamed x33, local copies, waits for them, and re-layouts  19.5 us
    convert_element_type x7, local copies, waits for them, and re-layouts, expand(): return jnp.repeat(jnp.repeat(mask, BLOCK, 0), BLOCK, 1).astype(jnp.bfloat16)  18.9 us
    dot_general x3, matrix products, contract_first(): lax.dot_general(left, right, (((0,), (0,)), ((), ())), preferred_element_...  18.7 us
    dot_general x3, matrix products, contract_last(): lax.dot_general(left, right, (((1,), (1,)), ((), ())), preferred_element_...  13.7 us
  transfers between devices with their start and end apart: 3, of which 3 were waited for; matrix products, arithmetic and copies ran while one was open for 25% of the time, Pallas kernels for 0%

commit v1 on v0

--- a/solution.py
+++ b/solution.py
@@ -37,7 +37,10 @@
     w_up = up_weight * keep_up
     w_down = down_weight * keep_down
     width = w_gate.shape[1]
-    pair = lax.all_gather(jnp.concatenate([tokens, cotangent], axis=1), "col", axis=0, tiled=True)
+    shard = jnp.concatenate([tokens, cotangent], axis=1)
+    size = lax.axis_size("col")
+    repeats = [size if d == 0 else 1 for d in range(shard.ndim)]
+    pair = lax.all_to_all(jnp.tile(shard, repeats), "col", split_axis=0, concat_axis=0, tiled=True)
     depth = tokens.shape[1]
     panel = pair[:, :depth]
     cot_panel = pair[:, depth:]

time: 290 us -> 329 us (1.13)
  waiting for transfers between devices: 102 us -> 126 us
  matrix products: 45.3 us -> 54.1 us
  starting transfers between devices: 7.65 us -> 15.9 us
  blocking collectives: 52.6 us -> 48.5 us
    all_to_all x0 -> x1, waiting for transfers between devices: none -> 48.8 us  [body(): lax.all_to_all(jnp.tile(shard, repeats), 'col', split_axis=0, concat_axis...]
    all_gather x1 -> x0, waiting for transfers between devices: 23.2 us -> none  [body(): lax.all_gather(jnp.concatenate([tokens, cotangent], axis=1), 'col', axis=...]
    all_to_all x0 -> x1, starting transfers between devices: none -> 8.52 us  [body(): lax.all_to_all(jnp.tile(shard, repeats), 'col', split_axis=0, concat_axis...]
    dot_general x3, matrix products: 18.7 us -> 23.4 us  [contract_first(): lax.dot_general(left, right, (((0,), (0,)), ((), ())), preferred_element_...]
    all_to_all x1, waiting for transfers between devices: 33.9 us -> 29.6 us  [body(): spread = lax.all_to_all(both, 'col', 0, 0, tiled=True)]
    all_to_all x1, blocking collectives: 52.6 us -> 48.5 us  [body(): swapped = lax.all_to_all(parts, 'row', 0, 0, tiled=True)]
    another operation x0 -> x1, local copies, waits for them, and re-layouts: none -> 3.41 us  [body(): jnp.tile(shard, repeats)]
    unnamed x33 -> x29, local copies, waits for them, and re-layouts: 19.5 us -> 19.5 us
  transfers between devices with their start and end apart: 3 -> 3, of which waited for: 3 -> 3; matrix products, arithmetic and copies ran while one was open for 25% -> 23% of each run, Pallas kernels for 0% -> 0%
where the time goes in v1:
time: 329 us; the launch traced here: 327 us
  waiting for transfers between devices  126 us (38%)
  matrix products  54.1 us (16%)
  local copies, waits for them, and re-layouts  49.4 us (15%)
  blocking collectives  48.5 us (15%)
  other arithmetic  19.6 us (6%)
  starting transfers between devices  15.9 us (5%)
  between operations  14.3 us (4%)
    all_to_all x1, waiting for transfers between devices, body(): lax.all_to_all(jnp.tile(shard, repeats), 'col', split_axis=0, concat_axis...  48.8 us
    all_to_all x1, blocking collectives, body(): swapped = lax.all_to_all(parts, 'row', 0, 0, tiled=True)  48.5 us
    all_gather x1, waiting for transfers between devices, body(): lax.all_gather(jnp.concatenate([hidden, dgate, dup], axis=1), 'row', axis...  47.4 us
    all_to_all x1, waiting for transfers between devices, body(): spread = lax.all_to_all(both, 'col', 0, 0, tiled=True)  29.6 us
    dot_general x3, matrix products, contract_first(): lax.dot_general(left, right, (((0,), (0,)), ((), ())), preferred_element_...  23.4 us
    unnamed x29, local copies, waits for them, and re-layouts  19.5 us
    convert_element_type x7, local copies, waits for them, and re-layouts, expand(): return jnp.repeat(jnp.repeat(mask, BLOCK, 0), BLOCK, 1).astype(jnp.bfloat16)  18.8 us
    dot_general x3, matrix products, contract_last(): lax.dot_general(left, right, (((1,), (1,)), ((), ())), preferred_element_...  13.7 us
  transfers between devices with their start and end apart: 3, of which 3 were waited for; matrix products, arithmetic and copies ran while one was open for 23% of the time, Pallas kernels for 0%

profile of v1, /device:TPU:0, one launch (start us, length us, event | category | flops | bytes accessed | tf_op | source)
XLA Modules:
  0.0 327.5 jit_solution(9567393655685182213)
XLA Ops:
  7.2 1.0 pad_maximum_fusion.3
  8.1 3.4 %tile.2 = bf16[32,24,4096]{2,1,0:T(8,128)(2,1)} broadcast(bf16[24,4096]{1,0:T(8,128)(2,1)S(1)} %pad_maximum_fusion.3), dimensions={1,2} | broadcast | bytes 6488064 | tf_op jit(solution)/shard_map/tile | solution.py:43
  11.5 8.5 %all-to-all-start = ((bf16[32,24,4096]{2,1,0:T(8,128)(2,1)}), bf16[32,24,4096]{2,1,0:T(8,128)(2,1)}, u32[]{:S(2)}, u32[]{:S(2)}) async-start(bf16[32,24,4096]{2,1,0:T(8,128)(2,1)} %tile.2), calls=%async_computation | async-start | bytes 12582912 | tf_op jit(solution)/shard_map/all_to_all | solution.py:43
  20.1 0.0 all-gather.2.cloned.1.call-start
  20.1 0.1 copy.24
  20.2 0.1 broadcast_in_dim.22
  20.4 0.1 convert_element_type.89
  20.5 6.1 %copy.25 = bf16[896,2048]{0,1:T(8,128)(2,1)} copy(bf16[896,2048]{1,0:T(8,128)(2,1)} %param.11) | data formatting | bytes 7340032 | tf_op args[3]
  26.6 0.1 broadcast_in_dim.20
  26.7 0.1 convert_element_type.85
  26.9 0.0 copy-start.10
  26.9 6.1 %copy.23 = bf16[2048,896]{0,1:T(8,128)(2,1)} copy(bf16[2048,896]{1,0:T(8,128)(2,1)} %param.10) | data formatting | bytes 7340032 | tf_op args[2]
  33.0 0.1 broadcast_in_dim.18
  33.1 0.1 convert_element_type.81
  33.2 6.1 %copy.22 = bf16[2048,896]{0,1:T(8,128)(2,1)} copy(bf16[2048,896]{1,0:T(8,128)(2,1)} %param.9) | data formatting | bytes 7340032 | tf_op args[1]
  39.3 4.4 %bitcast_multiply_fusion = bf16[896,2048]{0,1:T(8,128)(2,1)} fusion(bf16[896,2048]{0,1:T(8,128)(2,1)} %copy.25, bf16[896,32]{0,1:T(8,128)(2,1)S(1)} %convert_element_type.89), kind=kLoop, calls=%fused_computation.17 | loop fusion | flops 1835008 | bytes 7397376 | tf_op jit(solution)/shard_map/mul | solution.py:38
  43.7 2.1 bitcast_multiply_fusion.1
  45.8 1.2 copy-done.1
  47.1 2.1 bitcast_multiply_fusion.2
  49.2 48.8 %all-to-all-done = bf16[32,24,4096]{2,1,0:T(8,128)(2,1)} async-done(((bf16[32,24,4096]{2,1,0:T(8,128)(2,1)}), bf16[32,24,4096]{2,1,0:T(8,128)(2,1)}, u32[]{:S(2)}, u32[]{:S(2)}) %all-to-all-start) | async-done | bytes 6291488 | tf_op jit(solution)/shard_map/all_to_all | solution.py:43
  98.0 6.5 %fusion.15 = bf16[768,896]{1,0:T(8,128)(2,1)S(1)} fusion(bf16[896,2048]{0,1:T(8,128)(2,1)} %bitcast_multiply_fusion, bf16[768,4096]{1,0:T(8,128)(2,1)} %bitcast), kind=kOutput, calls=%fused_computation.22 | convolution fusion | flops 2819260416 | bytes 8192000 | tf_op jit(solution)/shard_map/dot_general | solution.py:14
  104.5 0.0 copy-start.4
  104.5 5.6 %fusion.12 = bf16[768,896]{1,0:T(8,128)(2,1)S(1)} fusion(bf16[2048,896]{0,1:T(8,128)(2,1)S(1)} %copy-done.2, bf16[768,4096]{1,0:T(8,128)(2,1)} %bitcast), kind=kOutput, calls=%fused_computation.21 | convolution fusion | flops 2819260416 | bytes 8192000 | tf_op jit(solution)/shard_map/dot_general | solution.py:50
  110.1 5.4 %fusion.9 = bf16[768,896]{1,0:T(8,128)(2,1)S(1)} fusion(bf16[2048,896]{0,1:T(8,128)(2,1)S(1)} %copy-done.4, bf16[768,4096]{1,0:T(8,128)(2,1)} %bitcast), kind=kOutput, calls=%fused_computation.20 | convolution fusion | flops 2819260416 | bytes 8192000 | tf_op jit(solution)/shard_map/dot_general | solution.py:49
  115.6 0.4 pad_maximum_fusion.1
  115.9 48.5 %all_to_all.27 = bf16[4,192,2688]{2,1,0:T(8,128)(2,1)S(1)} all-to-all(bf16[4,192,2688]{2,1,0:T(8,128)(2,1)S(1)} %bitcast.22), channel_id=1, replica_groups=mesh['row'=4,'col'=32] {'row'}, dimensions={0} | all-to-all | bytes 8257536 | tf_op jit(solution)/shard_map/all_to_all | solution.py:56
  164.4 0.6 convert_reduce_fusion
  165.1 0.4 multiply_convert_fusion.5
  165.5 1.1 pad_maximum_fusion.2
  166.5 0.0 all-gather.2.cloned.1.call-update
  166.6 47.4 %all-gather.2.cloned.1.call-done = bf16[768,2688]{1,0:T(8,128)(2,1)} async-done(((bf16[192,2688]{1,0:T(8,128)(2,1)}), bf16[768,2688]{1,0:T(8,128)(2,1)}) %all-gather.2.cloned.1.call-update) | async-done | bytes 4128784 | tf_op jit(solution)/shard_map/all_gather | solution.py:63
  213.9 6.0 %convolution_convert_fusion = bf16[768,2048]{1,0:T(8,128)(2,1)S(1)} fusion(bf16[896,2048]{0,1:T(8,128)(2,1)} %bitcast_multiply_fusion, bf16[768,2688]{1,0:T(8,128)(2,1)} %all-gather.2.cloned.1.call-done), kind=kOutput, calls=%fused_computation.7 | convolution fusion | flops 2820145152 | bytes 8192000 | tf_op jit(solution)/shard_map/dot_general | solution.py:69
  220.0 3.4 %fusion.21 = f32[768,2048]{1,0:T(8,128)S(1)} fusion(bf16[2048,896]{0,1:T(8,128)(2,1)S(1)} %copy-done.5, bf16[768,2688]{1,0:T(8,128)(2,1)S(1)} %copy-done.11), kind=kOutput, calls=%fused_computation.26 | convolution fusion | flops 2818572288 | bytes 11337728 | tf_op jit(solution)/shard_map/dot_general | solution.py:14
  223.4 3.7 %add_convert_fusion = bf16[768,2048]{1,0:T(8,128)(2,1)S(1)} fusion(f32[768,2048]{1,0:T(8,128)S(1)} %fusion.21, bf16[2048,896]{0,1:T(8,128)(2,1)S(1)} %copy-done.3, bf16[768,2688]{1,0:T(8,128)(2,1)S(1)} %copy-done.11), kind=kOutput, calls=%fused_computation.5 | convolution fusion | flops 2821718016 | bytes 14483456 | tf_op jit(solution)/shard_map/dot_general | solution.py:14
  227.2 3.4 %pad_maximum_fusion = bf16[768,4096]{1,0:T(8,128)(2,1)} fusion(bf16[768,2048]{1,0:T(8,128)(2,1)S(1)} %add_convert_fusion, bf16[768,2048]{1,0:T(8,128)(2,1)S(1)} %convolution_convert_fusion), kind=kLoop, calls=%fused_computation.4 | loop fusion | flops 12582912 | bytes 12582912 | tf_op jit(solution)/shard_map/concatenate | solution.py:67
  230.6 7.3 %all-to-all-start.2 = ((bf16[32,24,4096]{2,1,0:T(8,128)(2,1)}), bf16[32,24,4096]{2,1,0:T(8,128)(2,1)}, u32[]{:S(2)}, u32[]{:S(2)}) async-start(bf16[32,24,4096]{2,1,0:T(8,128)(2,1)} %bitcast.21), calls=%async_computation.2 | async-start | bytes 12582912 | tf_op jit(solution)/shard_map/all_to_all | solution.py:74
  237.9 2.1 broadcast_in_dim.23
  240.1 6.1 %copy.28 = bf16[896,2048]{1,0:T(8,128)(2,1)} copy(bf16[896,2048]{0,1:T(8,128)(2,1)} %bitcast.23) | data formatting | bytes 7340032 | tf_op jit(solution)/shard_map/convert_element_type | solution.py:10
  246.2 2.3 broadcast_in_dim.21
  248.5 6.0 %copy.27 = bf16[2048,896]{1,0:T(8,128)(2,1)} copy(bf16[2048,896]{0,1:T(8,128)(2,1)} %bitcast.24) | data formatting | bytes 7340032 | tf_op jit(solution)/shard_map/convert_element_type | solution.py:10
  254.5 2.3 broadcast_in_dim.19
  256.8 6.0 %copy.26 = bf16[2048,896]{1,0:T(8,128)(2,1)} copy(bf16[2048,896]{0,1:T(8,128)(2,1)} %bitcast.25) | data formatting | bytes 7340032 | tf_op jit(solution)/shard_map/convert_element_type | solution.py:10
  262.9 8.5 %multiply_convert_fusion = bf16[896,2048]{1,0:T(8,128)(2,1)} fusion(bf16[896,2048]{1,0:T(8,128)(2,1)} %copy.28, bf16[768,4096]{1,0:T(8,128)(2,1)} %bitcast, bf16[768,2688]{1,0:T(8,128)(2,1)} %all-gather.2.cloned.1.call-done), kind=kOutput, calls=%fused_computation.1 | convolution fusion | flops 2824077312 | bytes 11862016 | tf_op jit(solution)/shard_map/dot_general | solution.py:20
  271.4 7.5 %multiply_convert_fusion.1 = bf16[2048,896]{1,0:T(8,128)(2,1)} fusion(bf16[2048,896]{1,0:T(8,128)(2,1)S(1)} %copy-done.6, bf16[768,4096]{1,0:T(8,128)(2,1)} %bitcast, bf16[768,2688]{1,0:T(8,128)(2,1)S(1)} %copy-done.12), kind=kOutput, calls=%fused_computation.2 | convolution fusion | flops 2824077312 | bytes 11862016 | tf_op jit(solution)/shard_map/dot_general | solution.py:20
  278.9 7.4 %multiply_convert_fusion.2 = bf16[2048,896]{1,0:T(8,128)(2,1)} fusion(bf16[2048,896]{1,0:T(8,128)(2,1)S(1)} %copy-done.7, bf16[768,4096]{1,0:T(8,128)(2,1)} %bitcast, bf16[768,2688]{1,0:T(8,128)(2,1)S(1)} %copy-done.12), kind=kOutput, calls=%fused_computation.3 | convolution fusion | flops 2824077312 | bytes 11862016 | tf_op jit(solution)/shard_map/dot_general | solution.py:20
  286.3 29.6 %all-to-all-done.2 = bf16[32,24,4096]{2,1,0:T(8,128)(2,1)} async-done(((bf16[32,24,4096]{2,1,0:T(8,128)(2,1)}), bf16[32,24,4096]{2,1,0:T(8,128)(2,1)}, u32[]{:S(2)}, u32[]{:S(2)}) %all-to-all-start.2) | async-done | bytes 6291488 | tf_op jit(solution)/shard_map/all_to_all | solution.py:74
  315.8 4.1 %reduce_sum.22 = bf16[24,4096]{1,0:T(8,128)(2,1)S(1)} reduce(bf16[32,24,4096]{2,1,0:T(8,128)(2,1)} %all-to-all-done.2, bf16[]{:T(256)} %constant.7.clone.1), dimensions={0}, to_apply=%region_1.2 | reduce | flops 3047424 | bytes 6488066 | tf_op jit(solution)/shard_map/reduce_sum | solution.py:79
  319.9 0.7 fusion.25
  (26 shorter events, 0.1 us)
Async XLA Ops:
  11.5 8.6 %copy-start.8 = (s32[14,32]{1,0:T(8,128)S(1)}, s32[14,32]{1,0:T(8,128)}, u32[]{:S(2)}) copy-start(s32[14,32]{1,0:T(8,128)} %param.14) | copy-start | bytes 5380
  11.5 86.4 %all-to-all-start = ((bf16[32,24,4096]{2,1,0:T(8,128)(2,1)}), bf16[32,24,4096]{2,1,0:T(8,128)(2,1)}, u32[]{:S(2)}, u32[]{:S(2)}) async-start(bf16[32,24,4096]{2,1,0:T(8,128)(2,1)} %tile.2), calls=%async_computation | async-start | bytes 12582912 | tf_op jit(solution)/shard_map/all_to_all | solution.py:43
  20.1 193.9 %all-gather.2.cloned.1.call-start = ((), (), s32[]{:S(2)}) async-start(), calls=%async_computation.3 | async-start | bytes 5160960 | tf_op jit(solution)/shard_map/all_gather | solution.py:63
  20.5 6.1 %copy-start.9 = (s32[32,14]{0,1:T(8,128)S(1)}, s32[32,14]{0,1:T(8,128)}, u32[]{:S(2)}) copy-start(s32[32,14]{0,1:T(8,128)} %param.13) | copy-start | bytes 5380
  26.9 6.1 %copy-start.10 = (s32[32,14]{0,1:T(8,128)S(1)}, s32[32,14]{0,1:T(8,128)}, u32[]{:S(2)}) copy-start(s32[32,14]{0,1:T(8,128)} %param.12) | copy-start | bytes 5380
  39.3 4.4 %copy-start = (bf16[2048,896]{0,1:T(8,128)(2,1)S(1)}, bf16[2048,896]{0,1:T(8,128)(2,1)}, u32[]{:S(2)}) copy-start(bf16[2048,896]{0,1:T(8,128)(2,1)} %copy.23) | copy-start | bytes 11010052
  43.7 3.4 %copy-start.1 = (bf16[2048,896]{0,1:T(8,128)(2,1)S(1)}, bf16[2048,896]{0,1:T(8,128)(2,1)}, u32[]{:S(2)}) copy-start(bf16[2048,896]{0,1:T(8,128)(2,1)} %copy.22) | copy-start | bytes 11010052
  98.0 6.5 %copy-start.2 = (bf16[2048,896]{0,1:T(8,128)(2,1)S(1)}, bf16[2048,896]{0,1:T(8,128)(2,1)}, u32[]{:S(2)}) copy-start(bf16[2048,896]{0,1:T(8,128)(2,1)} %bitcast_multiply_fusion.1) | copy-start | bytes 11010052
  104.5 5.6 %copy-start.4 = (bf16[2048,896]{0,1:T(8,128)(2,1)S(1)}, bf16[2048,896]{0,1:T(8,128)(2,1)}, u32[]{:S(2)}) copy-start(bf16[2048,896]{0,1:T(8,128)(2,1)} %bitcast_multiply_fusion.2) | copy-start | bytes 11010052
  213.9 6.1 %copy-start.5 = (bf16[2048,896]{0,1:T(8,128)(2,1)S(1)}, bf16[2048,896]{0,1:T(8,128)(2,1)}, u32[]{:S(2)}) copy-start(bf16[2048,896]{0,1:T(8,128)(2,1)} %bitcast_multiply_fusion.2) | copy-start | bytes 11010052
  213.9 6.1 %copy-start.11 = (bf16[768,2688]{1,0:T(8,128)(2,1)S(1)}, bf16[768,2688]{1,0:T(8,128)(2,1)}, u32[]{:S(2)}) copy-start(bf16[768,2688]{1,0:T(8,128)(2,1)} %all-gather.2.cloned.1.call-done) | copy-start | bytes 12386308
  220.0 3.4 %copy-start.3 = (bf16[2048,896]{0,1:T(8,128)(2,1)S(1)}, bf16[2048,896]{0,1:T(8,128)(2,1)}, u32[]{:S(2)}) copy-start(bf16[2048,896]{0,1:T(8,128)(2,1)} %bitcast_multiply_fusion.1) | copy-start | bytes 11010052
  230.6 85.2 %all-to-all-start.2 = ((bf16[32,24,4096]{2,1,0:T(8,128)(2,1)}), bf16[32,24,4096]{2,1,0:T(8,128)(2,1)}, u32[]{:S(2)}, u32[]{:S(2)}) async-start(bf16[32,24,4096]{2,1,0:T(8,128)(2,1)} %bitcast.21), calls=%async_computation.2 | async-start | bytes 12582912 | tf_op jit(solution)/shard_map/all_to_all | solution.py:74
  262.9 8.5 %copy-start.6 = (bf16[2048,896]{1,0:T(8,128)(2,1)S(1)}, bf16[2048,896]{1,0:T(8,128)(2,1)}, u32[]{:S(2)}) copy-start(bf16[2048,896]{1,0:T(8,128)(2,1)} %copy.27) | copy-start | bytes 11010052
  262.9 8.5 %copy-start.12 = (bf16[768,2688]{1,0:T(8,128)(2,1)S(1)}, bf16[768,2688]{1,0:T(8,128)(2,1)}, u32[]{:S(2)}) copy-start(bf16[768,2688]{1,0:T(8,128)(2,1)} %all-gather.2.cloned.1.call-done) | copy-start | bytes 12386308
  271.3 7.5 %copy-start.7 = (bf16[2048,896]{1,0:T(8,128)(2,1)S(1)}, bf16[2048,896]{1,0:T(8,128)(2,1)}, u32[]{:S(2)}) copy-start(bf16[2048,896]{1,0:T(8,128)(2,1)} %copy.26) | copy-start | bytes 11010052
Sparse Core Ops, SparseCore 0:
  166.7 47.1 all-gather.1
